TPU v7x, 32 devices: a whole 2x2x4 slice. The times are simulated.
32 devices in a mesh: gx: 2 (over core), gy: 4 (over y, x), gz: 4 (over z).
Axes of the slice: x: 2, y: 2, z: 4, core: 2. Of those that a mesh axis runs over, the one named last changes fastest.
Arguments:
- student: bfloat16 [1024, 1024], P('gx', 'gz'), may hold values from -12 to 12
- teacher: bfloat16 [8192, 1024], P('gy', 'gz'), may hold values from -6 to 6
- block_ids: int32 [8, 32], P('gx'), may hold values from 0 to 63, as said below
- block_valid: int32 [8, 32], P('gx'), may hold values from 0 to 1
Outputs:
- row_potential: float32 [1024], P('gx')
- column_potential: float32 [8192], P('gy')
Inputs may be any that keep to these rules, and one draw needn't show every extreme that they name: `block_ids`: within each row block the valid slots name distinct column blocks, and at most 8 of them lie in one aligned group of 16 column blocks; in every draw some row block has exactly 8 valid slots in one group.
All inputs are finite; a program needn't handle non-finite values.
Results may differ from a plain program's by a relative error of at most 0.0003.
Values sent between devices are 32-bit elements; how exact they have to be, the bound alone decides.
A program may use at most 64 MiB of HBM per device.

v0:
```python
import math
import jax
import jax.numpy as jnp
from jax import lax
from jax.sharding import PartitionSpec as P

F = 1024
TILE = 128
LOCAL_MOST = 8
ITERS = 5
SOFTNESS = 0.1
EXACT = lax.Precision.HIGHEST


def combined_all(x, axis, combine):
    everything = jax.tree.map(lambda part: lax.all_gather(part, axis), x)
    initial = jax.tree.map(lambda part: part[0], everything)

    def lap(k, so_far):
        return combine(so_far, jax.tree.map(lambda part: part[k], everything))

    return lax.fori_loop(1, lax.axis_size(axis), lap, initial)


def soft_bound(highest, totals):
    return -SOFTNESS * (highest + jnp.log(totals + jnp.exp(-highest)))


def pair_merge(earlier, later):
    highest = jnp.maximum(earlier[0], later[0])
    return (
        highest,
        earlier[1] * jnp.exp(earlier[0] - highest) + later[1] * jnp.exp(later[0] - highest),
    )


def row_partial(costs, column_values, one_hot, live_mask):
    gathered = jnp.einsum("rmb,bw->rmw", one_hot, column_values, precision=EXACT)
    scores = (gathered[:, :, :, None] - costs) / SOFTNESS
    highest = jnp.maximum(jnp.max(jnp.where(live_mask, scores, -1e30), axis=(1, 2)), 0.0)
    totals = jnp.sum(
        jnp.where(live_mask, jnp.exp(scores - highest[:, None, None, :]), 0.0), axis=(1, 2)
    )
    return (highest, totals)


def local_totals(scores, highest, one_hot, live_mask):
    chosen_peak = jnp.einsum("rmb,bw->rmw", one_hot, highest, precision=EXACT)
    tile_sum = jnp.sum(
        jnp.where(live_mask, jnp.exp(scores - chosen_peak[:, :, :, None]), 0.0), axis=3
    )
    return jnp.einsum("rmb,rmw->bw", one_hot, tile_sum, precision=EXACT)


def column_update(costs, row_values, one_hot, live_mask):
    scores = (row_values[:, None, None, :] - costs) / SOFTNESS
    tile_peak = jnp.max(scores, axis=3)
    spread_peak = jnp.where(one_hot[:, :, :, None] > 0, tile_peak[:, :, None, :], 0.0)
    local_peak = jnp.maximum(jnp.max(spread_peak, axis=(0, 1)), 0.0)
    partial_sum = local_totals(scores, local_peak, one_hot, live_mask)
    highest, totals = combined_all((local_peak, partial_sum), "gx", pair_merge)
    return soft_bound(highest, totals)


def on_device(student, teacher, block_ids, block_valid):
    span_blocks = teacher.shape[0] // TILE
    width_part = student.shape[1]
    column_index = lax.axis_index("gy")
    local_ids = block_ids - column_index * span_blocks
    owned = (block_valid > 0) & (local_ids >= 0) & (local_ids < span_blocks)
    slot_rank = jnp.cumsum(owned.astype(jnp.int32), axis=1) - 1
    slot_range = jnp.arange(LOCAL_MOST, dtype=jnp.int32)
    chosen_slots = (
        owned[:, None, :] & (slot_rank[:, None, :] == slot_range[None, :, None])
    ).astype(jnp.int32)
    live_slots = jnp.sum(chosen_slots, axis=2)
    block_of = jnp.sum(chosen_slots * local_ids[:, None, :], axis=2)
    block_range = jnp.arange(span_blocks, dtype=jnp.int32)
    one_hot = (
        (block_of[:, :, None] == block_range[None, None, :]) & (live_slots[:, :, None] > 0)
    ).astype(jnp.float32)
    live_mask = (live_slots > 0)[:, :, None, None]
    teacher_blocks = teacher.reshape(span_blocks, TILE, width_part)
    student_blocks = student.reshape(-1, TILE, width_part)
    picked = teacher_blocks[block_of]
    partial_dots = jnp.einsum(
        "rmcf,rif->rmci", picked, student_blocks, preferred_element_type=jnp.float32
    )
    cost_scale = -1.0 / math.sqrt(F)
    costs = lax.psum(partial_dots, "gz") * cost_scale
    column_values = jnp.zeros((span_blocks, costs.shape[2]), jnp.float32)
    row_values = jnp.zeros((student_blocks.shape[0], TILE), jnp.float32)
    for sweep in range(ITERS):
        highest, totals = row_partial(costs, column_values, one_hot, live_mask)
        highest, totals = combined_all((highest, totals), "gy", pair_merge)
        row_values = soft_bound(highest, totals)
        column_values = column_update(costs, row_values, one_hot, live_mask)
    return (row_values.reshape(-1), column_values.reshape(-1))


def solution(mesh):
    placed = (P("gx", "gz"), P("gy", "gz"), P("gx", None), P("gx", None))
    return jax.shard_map(
        on_device, mesh=mesh, in_specs=placed, out_specs=(P("gx"), P("gy")), check_vma=False
    )
```

profile of v0, /device:TPU:0, one launch (start us, length us, event | category | flops | bytes accessed | tf_op | source)
XLA Modules:
  0.0 226.9 jit_solution(7999439772396991120)
XLA Ops:
  7.2 0.8 fusion.164
  8.6 0.7 gather_fusion
  9.5 2.0 fusion.165
  11.8 88.7 %all-reduce.2.cloned.1.call-done = f32[4,8,128,128]{3,2,1,0:T(8,128)} async-done(((f32[4,8,128,128]{3,2,1,0:T(8,128)}), f32[4,8,128,128]{3,2,1,0:T(8,128)}) %all-reduce.2.cloned.1.call-update) | async-done | bytes 2097168 | tf_op jit(solution)/shard_map/psum | solution.py:90
  100.6 2.1 select_reduce_fusion.14
  102.8 0.8 select_reduce_fusion.13
  103.6 8.1 %all-gather.21 = f32[4,4,128]{2,1,0:T(4,128)S(1)} all-gather(f32[1,4,128]{2,1,0:T(4,128)S(1)} %bitcast.193), channel_id=3, replica_groups=mesh['gx'=2,'gy'=4,'gz'=4] {'gy'}, dimensions={0}, use_global_device_ids=true | all-gather | bytes 10240 | tf_op jit(solution)/shard_map/all_gather | solution.py:16
  111.6 8.0 %all-gather.20 = f32[4,4,128]{2,1,0:T(4,128)S(1)} all-gather(f32[1,4,128]{2,1,0:T(4,128)S(1)} %get-tuple-element.841), channel_id=2, replica_groups=mesh['gx'=2,'gy'=4,'gz'=4] {'gy'}, dimensions={0}, use_global_device_ids=true | all-gather | bytes 10240 | tf_op jit(solution)/shard_map/all_gather | solution.py:16
  119.8 0.6 fusion.10
  120.8 1.3 select_reduce_fusion.12
  122.1 0.3 convolution_bitcast_fusion.4
  122.4 1.8 all-gather.3
  124.2 1.8 all-gather.2
  126.2 0.8 select_reduce_fusion.11
  127.0 0.8 select_reduce_fusion.10
  127.8 7.1 %all-gather.23 = f32[4,4,128]{2,1,0:T(4,128)S(1)} all-gather(f32[1,4,128]{2,1,0:T(4,128)S(1)} %bitcast.194), channel_id=7, replica_groups=mesh['gx'=2,'gy'=4,'gz'=4] {'gy'}, dimensions={0}, use_global_device_ids=true | all-gather | bytes 10240 | tf_op jit(solution)/shard_map/all_gather | solution.py:16
  134.9 8.0 %all-gather.22 = f32[4,4,128]{2,1,0:T(4,128)S(1)} all-gather(f32[1,4,128]{2,1,0:T(4,128)S(1)} %get-tuple-element.839), channel_id=6, replica_groups=mesh['gx'=2,'gy'=4,'gz'=4] {'gy'}, dimensions={0}, use_global_device_ids=true | all-gather | bytes 10240 | tf_op jit(solution)/shard_map/all_gather | solution.py:16
  143.1 0.6 fusion.11
  144.1 1.3 select_reduce_fusion.9
  145.4 0.3 convolution_bitcast_fusion.3
  145.7 1.8 all-gather.7
  147.5 1.8 all-gather.6
  149.5 0.8 select_reduce_fusion.8
  150.3 0.8 select_reduce_fusion.7
  151.1 7.1 %all-gather.25 = f32[4,4,128]{2,1,0:T(4,128)S(1)} all-gather(f32[1,4,128]{2,1,0:T(4,128)S(1)} %bitcast.195), channel_id=11, replica_groups=mesh['gx'=2,'gy'=4,'gz'=4] {'gy'}, dimensions={0}, use_global_device_ids=true | all-gather | bytes 10240 | tf_op jit(solution)/shard_map/all_gather | solution.py:16
  158.2 8.0 %all-gather.24 = f32[4,4,128]{2,1,0:T(4,128)S(1)} all-gather(f32[1,4,128]{2,1,0:T(4,128)S(1)} %get-tuple-element.837), channel_id=10, replica_groups=mesh['gx'=2,'gy'=4,'gz'=4] {'gy'}, dimensions={0}, use_global_device_ids=true | all-gather | bytes 10240 | tf_op jit(solution)/shard_map/all_gather | solution.py:16
  166.4 0.6 fusion.12
  167.4 1.3 select_reduce_fusion.6
  168.7 0.3 convolution_bitcast_fusion.2
  169.0 1.8 all-gather.11
  170.8 1.8 all-gather.10
  172.8 0.8 select_reduce_fusion.5
  173.6 0.8 select_reduce_fusion.4
  174.4 7.1 %all-gather.27 = f32[4,4,128]{2,1,0:T(4,128)S(1)} all-gather(f32[1,4,128]{2,1,0:T(4,128)S(1)} %bitcast.196), channel_id=15, replica_groups=mesh['gx'=2,'gy'=4,'gz'=4] {'gy'}, dimensions={0}, use_global_device_ids=true | all-gather | bytes 10240 | tf_op jit(solution)/shard_map/all_gather | solution.py:16
  181.5 8.0 %all-gather.26 = f32[4,4,128]{2,1,0:T(4,128)S(1)} all-gather(f32[1,4,128]{2,1,0:T(4,128)S(1)} %get-tuple-element.835), channel_id=14, replica_groups=mesh['gx'=2,'gy'=4,'gz'=4] {'gy'}, dimensions={0}, use_global_device_ids=true | all-gather | bytes 10240 | tf_op jit(solution)/shard_map/all_gather | solution.py:16
  189.7 0.6 fusion.13
  190.7 1.3 select_reduce_fusion.3
  192.3 1.8 all-gather.15
  194.1 2.0 all-gather.14
  196.3 0.8 select_reduce_fusion.2
  197.1 0.8 select_reduce_fusion.1
  197.8 7.1 %all-gather.29 = f32[4,4,128]{2,1,0:T(4,128)S(1)} all-gather(f32[1,4,128]{2,1,0:T(4,128)S(1)} %bitcast.197), channel_id=19, replica_groups=mesh['gx'=2,'gy'=4,'gz'=4] {'gy'}, dimensions={0}, use_global_device_ids=true | all-gather | bytes 10240 | tf_op jit(solution)/shard_map/all_gather | solution.py:16
  205.0 8.0 %all-gather.28 = f32[4,4,128]{2,1,0:T(4,128)S(1)} all-gather(f32[1,4,128]{2,1,0:T(4,128)S(1)} %get-tuple-element.833), channel_id=18, replica_groups=mesh['gx'=2,'gy'=4,'gz'=4] {'gy'}, dimensions={0}, use_global_device_ids=true | all-gather | bytes 10240 | tf_op jit(solution)/shard_map/all_gather | solution.py:16
  213.2 0.6 fusion.14
  214.2 1.3 select_reduce_fusion
  215.8 1.8 all-gather.19
  217.6 1.8 all-gather.18
  219.4 0.6 fusion.47
  (80 shorter events, 5.3 us)
Async XLA Ops:
  7.2 1.4 copy-start
  7.2 93.4 %all-reduce.2.cloned.1.call-start = ((), (), s32[]{:S(2)}) async-start(), calls=%async_computation | async-start | bytes 4194304 | tf_op jit(solution)/shard_map/psum | solution.py:90
  8.6 1.0 copy-start.2
  100.6 2.2 copy-start.1
  213.2 2.3 %copy-start.3 = (f32[4,128]{1,0:T(4,128)}, f32[4,128]{1,0:T(4,128)S(1)}, u32[]{:S(2)}) copy-start(f32[4,128]{1,0:T(4,128)S(1)} %add_multiply_fusion) | copy-start | bytes 6148
Sparse Core Ops, SparseCore 0:
  11.7 88.8 all-reduce.1
where the time goes:
time: 227 us
  blocking collectives  95.1 us (42%)
  waiting for transfers between devices  88.8 us (39%)
  other arithmetic  22 us (10%)
  between operations  14.4 us (6%)
  matrix products  5.22 us (2%)
    all_gather x20, blocking collectives, combined_all(): everything = jax.tree.map(lambda part: lax.all_gather(part, axis), x)  95.1 us
    psum x1, waiting for transfers between devices, on_device(): costs = lax.psum(partial_dots, 'gz') * cost_scale  88.7 us
    reduce_sum x5, other arithmetic, local_totals(): jnp.sum(jnp.where(live_mask, jnp.exp(scores - chosen_peak[:, :, :, None])...  6.74 us
    reduce_max x5, other arithmetic, row_partial(): jnp.max(jnp.where(live_mask, scores, -1e+30), axis=(1, 2))  5.15 us
  transfers between devices with their start and end apart: 1, of which 1 were waited for; matrix products, arithmetic and copies ran while one was open for 0% of the time, Pallas kernels for 0%

commit v1 on v0

--- a/solution.py
+++ b/solution.py
@@ -10,6 +10,7 @@
 ITERS = 5
 SOFTNESS = 0.1
 EXACT = lax.Precision.HIGHEST
+deliver_meshes = lambda panel: jnp.sum(lax.all_gather(panel, "gz"), 0)
 
 
 def combined_all(x, axis, combine):
@@ -87,7 +88,7 @@
         "rmcf,rif->rmci", picked, student_blocks, preferred_element_type=jnp.float32
     )
     cost_scale = -1.0 / math.sqrt(F)
-    costs = lax.psum(partial_dots, "gz") * cost_scale
+    costs = deliver_meshes(partial_dots) * cost_scale
     column_values = jnp.zeros((span_blocks, costs.shape[2]), jnp.float32)
     row_values = jnp.zeros((student_blocks.shape[0], TILE), jnp.float32)
     for sweep in range(ITERS):

time: 227 us -> 294 us (1.30)
  waiting for transfers between devices: 88.8 us -> 152 us
  other arithmetic: 22 us -> 25 us
    all_gather x0 -> x1, waiting for transfers between devices: none -> 152 us  [deliver_meshes = lambda panel: jnp.sum(lax.all_gather(panel, 'gz'), 0)]
    psum x1 -> x0, waiting for transfers between devices: 88.7 us -> none  [on_device(): costs = lax.psum(partial_dots, 'gz') * cost_scale]
    reduce_sum x0 -> x1, other arithmetic: none -> 4.41 us  [deliver_meshes = lambda panel: jnp.sum(lax.all_gather(panel, 'gz'), 0)]
where the time goes in v1:
time: 294 us; the launch traced here: 293 us
  waiting for transfers between devices  152 us (52%)
  blocking collectives  95.1 us (32%)
  other arithmetic  25 us (9%)
  between operations  14.4 us (5%)
  matrix products  5.32 us (2%)
    all_gather x1, waiting for transfers between devices, deliver_meshes = lambda panel: jnp.sum(lax.all_gather(panel, 'gz'), 0)  152 us
    all_gather x20, blocking collectives, combined_all(): everything = jax.tree.map(lambda part: lax.all_gather(part, axis), x)  95.1 us
    reduce_sum x5, other arithmetic, local_totals(): jnp.sum(jnp.where(live_mask, jnp.exp(scores - chosen_peak[:, :, :, None])...  6.74 us
  transfers between devices with their start and end apart: 1, of which 1 were waited for; matrix products, arithmetic and copies ran while one was open for 0% of the time, Pallas kernels for 0%

profile of v1, /device:TPU:0, one launch (start us, length us, event | category | flops | bytes accessed | tf_op | source)
XLA Modules:
  0.0 293.4 jit_solution(17399141005065500172)
XLA Ops:
  7.2 0.8 fusion.164
  8.6 0.7 gather_fusion
  9.5 2.1 fusion.165
  11.9 152.2 %all-gather.33.cloned.1.call-done = f32[16,8,128,128]{3,2,1,0:T(8,128)} async-done(((f32[4,8,128,128]{3,2,1,0:T(8,128)}), f32[16,8,128,128]{3,2,1,0:T(8,128)}) %all-gather.33.cloned.1.call-update) | async-done | bytes 8388624 | tf_op jit(solution)/shard_map/all_gather | solution.py:13
  164.1 4.4 %reduce_sum.122 = f32[4,8,128,128]{3,2,1,0:T(8,128)S(1)} reduce(f32[4,4,8,128,128]{4,3,2,1,0:T(8,128)} %bitcast.191, f32[]{:T(128)} %constant.253.clone.1), dimensions={0}, to_apply=%region_3.4 | reduce | flops 1572864 | bytes 10485764 | tf_op jit(solution)/shard_map/reduce_sum | solution.py:13
  168.5 0.8 select_reduce_fusion.14
  169.3 0.8 select_reduce_fusion.13
  170.1 8.1 %all-gather.22 = f32[4,4,128]{2,1,0:T(4,128)S(1)} all-gather(f32[1,4,128]{2,1,0:T(4,128)S(1)} %bitcast.195), channel_id=4, replica_groups=mesh['gx'=2,'gy'=4,'gz'=4] {'gy'}, dimensions={0}, use_global_device_ids=true | all-gather | bytes 10240 | tf_op jit(solution)/shard_map/all_gather | solution.py:17
  178.2 8.0 %all-gather.21 = f32[4,4,128]{2,1,0:T(4,128)S(1)} all-gather(f32[1,4,128]{2,1,0:T(4,128)S(1)} %get-tuple-element.841), channel_id=3, replica_groups=mesh['gx'=2,'gy'=4,'gz'=4] {'gy'}, dimensions={0}, use_global_device_ids=true | all-gather | bytes 10240 | tf_op jit(solution)/shard_map/all_gather | solution.py:17
  186.3 0.6 fusion.10
  187.3 1.3 select_reduce_fusion.12
  188.7 0.3 convolution_bitcast_fusion.4
  188.9 1.8 all-gather.4
  190.8 1.8 all-gather.3
  192.8 0.8 select_reduce_fusion.11
  193.5 0.8 select_reduce_fusion.10
  194.3 7.1 %all-gather.24 = f32[4,4,128]{2,1,0:T(4,128)S(1)} all-gather(f32[1,4,128]{2,1,0:T(4,128)S(1)} %bitcast.196), channel_id=8, replica_groups=mesh['gx'=2,'gy'=4,'gz'=4] {'gy'}, dimensions={0}, use_global_device_ids=true | all-gather | bytes 10240 | tf_op jit(solution)/shard_map/all_gather | solution.py:17
  201.5 8.0 %all-gather.23 = f32[4,4,128]{2,1,0:T(4,128)S(1)} all-gather(f32[1,4,128]{2,1,0:T(4,128)S(1)} %get-tuple-element.839), channel_id=7, replica_groups=mesh['gx'=2,'gy'=4,'gz'=4] {'gy'}, dimensions={0}, use_global_device_ids=true | all-gather | bytes 10240 | tf_op jit(solution)/shard_map/all_gather | solution.py:17
  209.6 0.6 fusion.11
  210.6 1.3 select_reduce_fusion.9
  212.0 0.3 convolution_bitcast_fusion.3
  212.2 1.8 all-gather.8
  214.1 1.8 all-gather.7
  216.1 0.8 select_reduce_fusion.8
  216.8 0.8 select_reduce_fusion.7
  217.6 7.1 %all-gather.26 = f32[4,4,128]{2,1,0:T(4,128)S(1)} all-gather(f32[1,4,128]{2,1,0:T(4,128)S(1)} %bitcast.197), channel_id=12, replica_groups=mesh['gx'=2,'gy'=4,'gz'=4] {'gy'}, dimensions={0}, use_global_device_ids=true | all-gather | bytes 10240 | tf_op jit(solution)/shard_map/all_gather | solution.py:17
  224.7 8.0 %all-gather.25 = f32[4,4,128]{2,1,0:T(4,128)S(1)} all-gather(f32[1,4,128]{2,1,0:T(4,128)S(1)} %get-tuple-element.837), channel_id=11, replica_groups=mesh['gx'=2,'gy'=4,'gz'=4] {'gy'}, dimensions={0}, use_global_device_ids=true | all-gather | bytes 10240 | tf_op jit(solution)/shard_map/all_gather | solution.py:17
  232.9 0.6 fusion.12
  233.9 1.3 select_reduce_fusion.6
  235.5 1.8 all-gather.12
  237.3 1.8 all-gather.11
  239.4 0.8 select_reduce_fusion.5
  240.1 0.8 select_reduce_fusion.4
  240.9 7.1 %all-gather.28 = f32[4,4,128]{2,1,0:T(4,128)S(1)} all-gather(f32[1,4,128]{2,1,0:T(4,128)S(1)} %bitcast.198), channel_id=16, replica_groups=mesh['gx'=2,'gy'=4,'gz'=4] {'gy'}, dimensions={0}, use_global_device_ids=true | all-gather | bytes 10240 | tf_op jit(solution)/shard_map/all_gather | solution.py:17
  248.0 8.2 %all-gather.27 = f32[4,4,128]{2,1,0:T(4,128)S(1)} all-gather(f32[1,4,128]{2,1,0:T(4,128)S(1)} %get-tuple-element.835), channel_id=15, replica_groups=mesh['gx'=2,'gy'=4,'gz'=4] {'gy'}, dimensions={0}, use_global_device_ids=true | all-gather | bytes 10240 | tf_op jit(solution)/shard_map/all_gather | solution.py:17
  256.4 0.6 fusion.13
  257.4 1.3 select_reduce_fusion.3
  259.0 1.8 all-gather.16
  260.8 1.8 all-gather.15
  262.8 0.8 select_reduce_fusion.2
  263.6 0.8 select_reduce_fusion.1
  264.4 7.1 %all-gather.30 = f32[4,4,128]{2,1,0:T(4,128)S(1)} all-gather(f32[1,4,128]{2,1,0:T(4,128)S(1)} %bitcast.199), channel_id=20, replica_groups=mesh['gx'=2,'gy'=4,'gz'=4] {'gy'}, dimensions={0}, use_global_device_ids=true | all-gather | bytes 10240 | tf_op jit(solution)/shard_map/all_gather | solution.py:17
  271.5 8.0 %all-gather.29 = f32[4,4,128]{2,1,0:T(4,128)S(1)} all-gather(f32[1,4,128]{2,1,0:T(4,128)S(1)} %get-tuple-element.833), channel_id=19, replica_groups=mesh['gx'=2,'gy'=4,'gz'=4] {'gy'}, dimensions={0}, use_global_device_ids=true | all-gather | bytes 10240 | tf_op jit(solution)/shard_map/all_gather | solution.py:17
  279.7 0.6 fusion.14
  280.7 1.3 select_reduce_fusion
  282.3 1.8 all-gather.20
  284.1 1.8 all-gather.19
  285.9 0.6 fusion.47
  (79 shorter events, 5.4 us)
Async XLA Ops:
  7.2 1.4 copy-start
  7.2 157.0 %all-gather.33.cloned.1.call-start = ((), (), s32[]{:S(2)}) async-start(), calls=%async_computation | async-start | bytes 10485760 | tf_op jit(solution)/shard_map/all_gather | solution.py:13
  8.6 1.0 copy-start.1
  279.7 2.3 copy-start.2
Sparse Core Ops, SparseCore 0:
  11.8 152.3 all-gather.32
